TPU v7x, 256 devices: a whole 4x4x8 slice. The times are simulated.
256 devices in a mesh: depth: 32 (over x, z_lo, y), cols: 8 (over z_hi, core).
Axes of the slice: x: 4, y: 4, z: 8 (z_hi: 4, z_lo: 2; z = z_hi * 2 + z_lo), core: 2. Of those that a mesh axis runs over, the one named last changes fastest.
Arguments:
- amplitudes: float32 [2304, 32768], P('cols', 'depth'), may hold values from -6 to 6
- integrals: float32 [32768, 8192], P('depth', 'cols'), may hold values from -0.03125 to 0.03125
- residual_in: float32 [2304, 8192], P('depth', 'cols'), may hold values from -4 to 4
Outputs:
- residual_out: float32 [2304, 8192], P('depth', 'cols')
All inputs are finite; a program needn't handle non-finite values.
Results may differ from a plain program's by a relative error of at most 0.000071.
Values sent between devices are 32-bit elements; how exact they have to be, the bound alone decides.
A program may use at most 64 MiB of HBM per device.

v0:
```python
import jax
import jax.numpy as jnp
from jax import lax
from jax.sharding import PartitionSpec as P


def shards(amplitudes, integrals, residual_in):
    panel = lax.all_gather(amplitudes, "cols", axis=0, tiled=True)
    partial_value = jnp.dot(
        panel, integrals, precision=lax.Precision.HIGHEST, preferred_element_type=jnp.float32
    )
    owned = lax.psum_scatter(partial_value, "depth", scatter_dimension=0, tiled=True)
    return residual_in + owned


def solution(mesh):
    placed = (P("cols", "depth"), P("depth", "cols"), P("depth", "cols"))
    return jax.shard_map(
        shards, mesh=mesh, in_specs=placed, out_specs=P("depth", "cols"), check_vma=False
    )
```

profile of v0, /device:TPU:64, one launch (start us, length us, event | category | flops | bytes accessed | tf_op | source)
XLA Modules:
  0.0 334.9 jit_solution(11174748517182940044)
XLA Ops:
  6.5 0.0 all-gather.2.cloned.1.call-start
  6.5 0.7 all-gather.2.cloned.1.call-update
  7.3 0.0 reduce-scatter.2.cloned.1.call-start
  7.3 100.3 %all-gather.2.cloned.1.call-done = f32[2304,1024]{1,0:T(8,128)} async-done(((f32[288,1024]{1,0:T(8,128)}), f32[2304,1024]{1,0:T(8,128)}) %all-gather.2.cloned.1.call-update) | async-done | bytes 9437200 | tf_op jit(solution)/shard_map/all_gather | solution.py:8
  107.6 35.3 %fusion = f32[2304,1024]{1,0:T(8,128)} fusion(f32[2304,1024]{1,0:T(8,128)} %all-gather.2.cloned.1.call-done, f32[1024,1024]{1,0:T(8,128)} %param.4), kind=kOutput, calls=%fused_computation | convolution fusion | flops 28991029248 | bytes 23068672 | tf_op jit(solution)/shard_map/dot_general | solution.py:9
  142.9 0.0 copy-start
  142.9 0.0 reduce-scatter.2.cloned.1.call-update
  142.9 183.5 %reduce-scatter.2.cloned.1.call-done = f32[72,1024]{1,0:T(8,128)} async-done(((f32[2304,1024]{1,0:T(8,128)}), f32[72,1024]{1,0:T(8,128)}) %reduce-scatter.2.cloned.1.call-update) | async-done | bytes 294928 | tf_op jit(solution)/shard_map/reduce_scatter | solution.py:12
  326.4 0.0 copy-done
  326.4 1.7 add.5
Async XLA Ops:
  6.5 101.1 %all-gather.2.cloned.1.call-start = ((), (), s32[]{:S(2)}) async-start(), calls=%async_computation.1 | async-start | bytes 10616832 | tf_op jit(solution)/shard_map/all_gather | solution.py:8
  7.3 319.1 %reduce-scatter.2.cloned.1.call-start = ((), (), s32[]{:S(2)}) async-start(), calls=%async_computation.2 | async-start | bytes 9732096 | tf_op jit(solution)/shard_map/reduce_scatter | solution.py:12
  142.9 183.5 %copy-start = (f32[72,1024]{1,0:T(8,128)S(1)}, f32[72,1024]{1,0:T(8,128)}, u32[]{:S(2)}) copy-start(f32[72,1024]{1,0:T(8,128)} %param.5) | copy-start | bytes 884740
Sparse Core Ops, SparseCore 0:
  9.2 98.3 all-gather.1
  143.0 183.2 reduce-scatter.1
where the time goes:
time: 335 us
  waiting for transfers between devices  284 us (85%)
  matrix products  35.3 us (11%)
  between operations  13.4 us (4%)
    reduce_scatter x1, waiting for transfers between devices, shards(): lax.psum_scatter(partial_value, 'depth', scatter_dimension=0, tiled=True)  183 us
    all_gather x1, waiting for transfers between devices, shards(): panel = lax.all_gather(amplitudes, 'cols', axis=0, tiled=True)  100 us
    dot_general x1, matrix products, shards(): jnp.dot(panel, integrals, precision=lax.Precision.HIGHEST, preferred_elem...  35.3 us
  transfers between devices with their start and end apart: 2, of which 2 were waited for; matrix products, arithmetic and copies ran while one was open for 0% of the time, Pallas kernels for 0%

commit v1 on v0

v1 whole, which is shorter than its diff:
```python
import functools

import jax
import jax.numpy as jnp
from jax import lax
from jax.experimental import pallas as pl
from jax.experimental.pallas import tpu as pltpu
from jax.sharding import PartitionSpec as P

MESH = pl.DeviceIdType.MESH
R = 8
T = 72 // R
AHEAD = 2
K = 1024
NB = 512
PIECES = 4
HOPS = (1, -1, 2)


def kernel(a_ref, b_ref, o_ref, apan, bown, bsib, bh, bl, p1, p2, r1, r2, q1, q2, s1, s2, red, zr,
           own_sem, bown_sem, bs_sem, br_sem, ags, agr, fws, fwr, st1s, st1r, st2s, st2r, zs, zrs):
    d = lax.axis_index("depth")
    j = lax.axis_index("cols")
    x, zl, y = d // 8, (d // 4) % 2, d % 4
    zh, c = j // 2, j % 2

    def dev(x_, zl_, y_, zh_, c_):
        return (x_ * 8 + zl_ * 4 + y_, zh_ * 2 + c_)

    def ring(v, n):
        return (v + n + 4) % 4

    up = dev(x, zl, y, ring(zh, 1), c)
    down = dev(x, zl, y, ring(zh, -1), c)
    sib = dev(x, zl, y, zh, 1 - c)
    xs = [dev(ring(x, n), zl, y, zh, c) for n in HOPS]
    ys = [dev(x, zl, ring(y, n), zh, c) for n in HOPS]
    far = [dev(x, 1 - zl, y, zh, h) for h in range(2)]
    opp = ring(zh, 2)

    def rcopy(src, dst, ss, rs, to):
        return pltpu.make_async_remote_copy(
            src_ref=src, dst_ref=dst, send_sem=ss, recv_sem=rs, device_id=to, device_id_type=MESH
        )

    def own_copy(s):
        return pltpu.make_async_copy(a_ref.at[:, s], apan.at[s, zh], own_sem.at[s])

    bcopy = pltpu.make_async_copy(b_ref, bown, bown_sem)
    bcopy.start()

    peers = [up, down, sib] + xs + ys + far
    barrier = pltpu.get_barrier_semaphore()
    for peer in peers:
        pl.semaphore_signal(barrier, inc=1, device_id=peer, device_id_type=MESH)
    pl.semaphore_wait(barrier, len(peers))

    def ag(s, way):
        return rcopy(a_ref.at[:, s], apan.at[s, zh], ags.at[way, s], agr.at[way, s], (up, down)[way])

    def ag_in(s, way):
        blk = ring(zh, (-1, 1)[way])
        return rcopy(apan.at[s, blk], apan.at[s, blk], ags.at[way, s], agr.at[way, s], (up, down)[way])

    def fw(s, way):
        blk = ring(zh, (-1, 1)[way])
        part = pl.ds(2 * way, 2)
        return rcopy(apan.at[s, blk, part], apan.at[s, blk, part], fws.at[way, s], fwr.at[way, s],
                     (up, down)[way])

    def fw_in(s, way):
        part = pl.ds(2 * way, 2)
        return rcopy(apan.at[s, opp, part], apan.at[s, opp, part], fws.at[way, s], fwr.at[way, s],
                     (up, down)[way])

    def bs(i):
        rows = pl.ds(i * (K // PIECES), K // PIECES)
        return rcopy(b_ref.at[rows], bsib.at[rows], bs_sem.at[i], br_sem.at[i], sib)

    def st1(s, path, i):
        if path == 0:
            return rcopy(p1.at[s, ring(x, HOPS[i])], r1.at[s, i], st1s.at[0, i, s], st1r.at[0, i, s], xs[i])
        return rcopy(p2.at[s, :, ring(y, HOPS[i])], r2.at[s, i], st1s.at[1, i, s], st1r.at[1, i, s], ys[i])

    def st2(s, path, i):
        if path == 0:
            return rcopy(q1.at[s, ring(y, HOPS[i])], s1.at[s, i], st2s.at[0, i, s], st2r.at[0, i, s], ys[i])
        return rcopy(q2.at[s, ring(x, HOPS[i])], s2.at[s, i], st2s.at[1, i, s], st2r.at[1, i, s], xs[i])

    def zfar(s, h):
        return rcopy(red.at[h, s], zr.at[0, s], zs.at[h, s], zrs.at[0, s], far[h])

    def zsib(s):
        return rcopy(red.at[1 - c, s], zr.at[1, s], zs.at[0, s], zrs.at[1, s], sib)

    def zin(s, k):
        return rcopy(red.at[0, s], zr.at[k, s], zs.at[0, s], zrs.at[k, s], sib)

    for s in range(AHEAD):
        for way in range(2):
            ag(s, way).start()
    for i in range(PIECES):
        bs(i).start()

    @pl.loop(0, T)
    def _(s):
        own_copy(s).start()

    def split(src, i, half):
        rows = pl.ds(pl.multiple_of(i * 128, 128), 128)
        v = src[rows, :]
        hi = v.astype(jnp.bfloat16)
        lo = (v - hi.astype(jnp.float32)).astype(jnp.bfloat16)
        cols = pl.ds(pl.multiple_of(half * K, K), K)
        bh[rows, cols] = hi
        bl[rows, cols] = lo

    def pass_on(s):
        for way in range(2):
            ag_in(s, way).wait_recv()
            fw(s, way).start()

    pass_on(0)
    bcopy.wait()

    @pl.loop(0, K // 128)
    def _(i):
        split(bown, i, c)

    for i in range(PIECES):
        bs(i).wait_recv()

    @pl.loop(0, K // 128)
    def _(i):
        split(bsib, i, 1 - c)

    def multiply(s):
        a = apan[s].reshape(16 * R, K)
        hi = a.astype(jnp.bfloat16)
        lo = (a - hi.astype(jnp.float32)).astype(jnp.bfloat16)
        both = jnp.concatenate([hi, lo], axis=0)
        for n in range(2 * K // NB):
            cols = pl.ds(n * NB, NB)
            two = jnp.dot(both, bh[:, cols], preferred_element_type=jnp.float32)
            acc = jnp.dot(hi, bl[:, cols], preferred_element_type=jnp.float32)
            acc = (two[: 16 * R] + (two[16 * R :] + acc)).reshape(4, 4, R, NB)
            if n * NB < K:
                p1[s, :, :, :, n * NB : (n + 1) * NB] = acc
            else:
                p2[s, :, :, :, n * NB - K : (n + 1) * NB - K] = acc

    @pl.loop(0, T + 3)
    def _(s):
        @pl.when(s + AHEAD < T)
        def _():
            for way in range(2):
                ag(s + AHEAD, way).start()

        @pl.when(s + 1 < T)
        def _():
            pass_on(s + 1)

        @pl.when(s < T)
        def _():
            own_copy(s).wait()
            for way in range(2):
                fw_in(s, way).wait_recv()
            multiply(s)
            for i in range(3):
                for path in range(2):
                    st1(s, path, i).start()

        @pl.when((s >= 1) & (s < T + 1))
        def _():
            t = s - 1
            for path in range(2):
                for i in range(3):
                    st1(t, path, i).wait_recv()
            q1[t] = (p1[t, x] + r1[t, 0]) + (r1[t, 1] + r1[t, 2])
            q2[t] = (p2[t, :, y] + r2[t, 0]) + (r2[t, 1] + r2[t, 2])
            for i in range(3):
                for path in range(2):
                    st2(t, path, i).start()

        @pl.when((s >= 2) & (s < T + 2))
        def _():
            t = s - 2
            for path in range(2):
                for i in range(3):
                    st2(t, path, i).wait_recv()
            red[0, t] = (q1[t, y] + s1[t, 0]) + (s1[t, 1] + s1[t, 2])
            red[1, t] = (q2[t, x] + s2[t, 0]) + (s2[t, 1] + s2[t, 2])

            @pl.when(zl == c)
            def _():
                zsib(t).start()

            @pl.when(zl != c)
            def _():
                for h in range(2):
                    zfar(t, h).start()

        @pl.when(s >= 3)
        def _():
            t = s - 3
            zin(t, 0).wait_recv()

            @pl.when(zl == c)
            def _():
                o_ref[t] = red[c, t] + zr[0, t]

            @pl.when(zl != c)
            def _():
                zin(t, 1).wait_recv()
                o_ref[t] = zr[0, t] + zr[1, t]

    for i in range(PIECES):
        bs(i).wait_send()

    @pl.loop(0, T)
    def _(s):
        for way in range(2):
            ag(s, way).wait_send()
            fw(s, way).wait_send()
        for path in range(2):
            for i in range(3):
                st1(s, path, i).wait_send()
                st2(s, path, i).wait_send()

        @pl.when(zl == c)
        def _():
            zsib(s).wait_send()

        @pl.when(zl != c)
        def _():
            for h in range(2):
                zfar(s, h).wait_send()


def ladder(a, b):
    f32, bf16 = jnp.float32, jnp.bfloat16
    dma = pltpu.SemaphoreType.DMA
    return pl.pallas_call(
        kernel,
        out_shape=jax.ShapeDtypeStruct((T, R, K), f32),
        in_specs=[pl.BlockSpec(memory_space=pl.ANY)] * 2,
        out_specs=pl.BlockSpec(memory_space=pltpu.VMEM),
        scratch_shapes=[
            pltpu.VMEM((T, 4, 4, R, K), f32),
            pltpu.VMEM((K, K), f32),
            pltpu.VMEM((K, K), f32),
            pltpu.VMEM((K, 2 * K), bf16),
            pltpu.VMEM((K, 2 * K), bf16),
            pltpu.VMEM((T, 4, 4, R, K), f32),
            pltpu.VMEM((T, 4, 4, R, K), f32),
            pltpu.VMEM((T, 3, 4, R, K), f32),
            pltpu.VMEM((T, 3, 4, R, K), f32),
            pltpu.VMEM((T, 4, R, K), f32),
            pltpu.VMEM((T, 4, R, K), f32),
            pltpu.VMEM((T, 3, R, K), f32),
            pltpu.VMEM((T, 3, R, K), f32),
            pltpu.VMEM((2, T, R, K), f32),
            pltpu.VMEM((2, T, R, K), f32),
            dma((T,)), dma, dma((PIECES,)), dma((PIECES,)),
            dma((2, T)), dma((2, T)), dma((2, T)), dma((2, T)),
            dma((2, 3, T)), dma((2, 3, T)), dma((2, 3, T)), dma((2, 3, T)),
            dma((2, T)), dma((2, T)),
        ],
        cost_estimate=pl.CostEstimate(flops=2 * 1152 * 2048 * 1024 * 3, bytes_accessed=8 * 2**20, transcendentals=0),
        compiler_params=pltpu.CompilerParams(collective_id=0, has_side_effects=True, vmem_limit_bytes=60 * 2**20),
    )(a, b)


def shards(amplitudes, integrals, residual_in):
    owned = ladder(amplitudes.reshape(4, T, R, K), integrals)
    return residual_in + owned.reshape(72, K)


def solution(mesh):
    placed = (P("cols", "depth"), P("depth", "cols"), P("depth", "cols"))
    return jax.shard_map(
        shards, mesh=mesh, in_specs=placed, out_specs=P("depth", "cols"), check_vma=False
    )
```

time: 335 us -> 121 us (0.36)
  the two profiles are of different devices: /device:TPU:64 before, /device:TPU:1 now
where the time goes in v1:
time: 121 us
  Pallas kernels  119 us (98%)
  other arithmetic  1.71 us (1%)
    pallas_call x1, Pallas kernels, ladder(): pl.pallas_call(kernel, out_shape=jax.ShapeDtypeStruct((T, R, K), f32), in...  119 us

profile of v1, /device:TPU:1, one launch (start us, length us, event | category | flops | bytes accessed | tf_op | source)
XLA Modules:
  0.0 121.0 jit_solution(11340372935238902504)
XLA Ops:
  0.0 0.0 copy-start
  0.0 119.3 %shard_map.37 = f32[9,8,1024]{2,1,0:T(8,128)} custom-call(f32[4,9,8,1024]{3,2,1,0:T(8,128)} %bitcast.3, f32[1024,1024]{1,0:T(8,128)} %b_ref.1), custom_call_target="tpu_custom_call" | custom-call | flops 14495514624 | bytes 8388608 | tf_op jit(solution)/shard_map/pallas_call | solution.py:243
  119.3 0.0 copy-done
  119.3 1.7 %bitcast_add_fusion = f32[72,1024]{1,0:T(8,128)} fusion(f32[72,1024]{1,0:T(8,128)S(1)} %copy-done, f32[9,8,1024]{2,1,0:T(8,128)} %shard_map.37), kind=kLoop, calls=%fused_computation | loop fusion | flops 73728 | bytes 884736 | tf_op jit(solution)/shard_map/add | solution.py:276
Async XLA Ops:
  0.0 119.3 %copy-start = (f32[72,1024]{1,0:T(8,128)S(1)}, f32[72,1024]{1,0:T(8,128)}, u32[]{:S(2)}) copy-start(f32[72,1024]{1,0:T(8,128)} %param.5) | copy-start | bytes 884740

commit v2 on v0

v2 whole, which is shorter than its diff:
```python
import jax
import jax.numpy as jnp
from jax import lax
from jax.experimental import pallas as pl
from jax.experimental.pallas import tpu as pltpu
from jax.sharding import PartitionSpec as P

MESH = pl.DeviceIdType.MESH
K = 1024
R = 8
T = 72 // R
AHEAD = 2
UN = 2
W = K // UN
U = T * UN
LAG = 2
HELD = (T - 1) * UN - 3 * LAG
PIECES = 4
HOPS = (1, -1, 2)


def kernel(a_ref, b_ref, o_ref, apan, bown, bsib, bh, bl, both, p, ra, rbc, m, q, r2, red, zr,
           own_sem, bown_sem, bss, bsr, ags, agr, fws, fwr, as_, ar, bs_, cs, bcr, st2s, st2r, zs, zrs):
    d = lax.axis_index("depth")
    j = lax.axis_index("cols")
    x, zl, y = d // 8, (d // 4) % 2, d % 4
    zh, c = j // 2, j % 2

    def dev(x_, zl_, y_, zh_, c_):
        return (x_ * 8 + zl_ * 4 + y_, zh_ * 2 + c_)

    def ring(v, n):
        return (v + n + 4) % 4

    up = dev(x, zl, y, ring(zh, 1), c)
    down = dev(x, zl, y, ring(zh, -1), c)
    sib = dev(x, zl, y, zh, 1 - c)
    xs = [dev(ring(x, n), zl, y, zh, c) for n in HOPS]
    ys = [dev(x, zl, ring(y, n), zh, c) for n in HOPS]
    far = [dev(x, 1 - zl, y, zh, h) for h in range(2)]
    opp = ring(zh, 2)
    first, second = (xs, ys), (ys, xs)
    at1, at2 = (x, y), (y, x)

    def rcopy(src, dst, ss, rs, to):
        return pltpu.make_async_remote_copy(
            src_ref=src, dst_ref=dst, send_sem=ss, recv_sem=rs, device_id=to, device_id_type=MESH
        )

    def own_copy(s):
        return pltpu.make_async_copy(a_ref.at[:, s], apan.at[s, zh], own_sem.at[s])

    bcopy = pltpu.make_async_copy(b_ref, bown, bown_sem)
    bcopy.start()

    peers = [up, down, sib] + xs + ys + far
    barrier = pltpu.get_barrier_semaphore()
    for peer in peers:
        pl.semaphore_signal(barrier, inc=1, device_id=peer, device_id_type=MESH)
    pl.semaphore_wait(barrier, len(peers))

    def ag(s, way):
        return rcopy(a_ref.at[:, s], apan.at[s, zh], ags.at[way], agr.at[way, s], (up, down)[way])

    def ag_in(s, way):
        blk = ring(zh, (-1, 1)[way])
        return rcopy(apan.at[s, blk], apan.at[s, blk], ags.at[way], agr.at[way, s], (up, down)[way])

    def fw(s, way):
        blk = ring(zh, (-1, 1)[way])
        part = pl.ds(2 * way, 2)
        return rcopy(apan.at[s, blk, part], apan.at[s, blk, part], fws.at[way], fwr.at[s],
                     (up, down)[way])

    def fw_in(s):
        return rcopy(apan.at[s, opp], apan.at[s, opp], fws.at[0], fwr.at[s], up)

    def bs(i):
        rows = pl.ds(i * (K // PIECES), K // PIECES)
        return rcopy(b_ref.at[rows], bsib.at[rows], bss, bsr.at[i], sib)

    def send_a(u, k, w):
        return rcopy(p.at[u, k, ring(at1[k], 2), pl.ds(2 * w, 2)], ra.at[u, k, w], as_, ar.at[u], first[k][w])

    def send_b(u, k, w):
        return rcopy(p.at[u, k, ring(at1[k], HOPS[w]), pl.ds(2 - 2 * w, 2)], rbc.at[u, 0, k, w], bs_, bcr.at[u],
                     first[k][w])

    def send_c(u, k, w):
        return rcopy(m.at[u, k, w], rbc.at[u, 1, k, w], cs, bcr.at[u], first[k][w])

    def send_2(u, k, i):
        return rcopy(q.at[u, k, ring(at2[k], HOPS[i])], r2.at[u, k, i], st2s, st2r.at[u], second[k][i])

    def arrived(buf, sem):
        rcopy(buf, buf, ags.at[0], sem, up).wait_recv()

    def sent(buf, sem):
        rcopy(buf, buf, sem, agr.at[0, 0], up).wait_send()

    def zfar(u, h):
        return rcopy(red.at[u, h], zr.at[u, 0], zs, zrs.at[u], far[h])

    def zsib(u):
        return rcopy(red.at[u, 1 - c], zr.at[u, 1], zs, zrs.at[u], sib)

    PAIRS = [(k, w) for w in range(2) for k in range(2)]

    for s in range(AHEAD):
        for way in range(2):
            ag(s, way).start()
    for i in range(PIECES):
        bs(i).start()

    @pl.loop(0, T)
    def _(s):
        own_copy(s).start()

    def split(src, i, half):
        rows = pl.ds(pl.multiple_of(i * 128, 128), 128)
        v = src[rows, :]
        hi = v.astype(jnp.bfloat16)
        lo = (v - hi.astype(jnp.float32)).astype(jnp.bfloat16)
        cols = pl.ds(pl.multiple_of(half * K, K), K)
        bh[rows, cols] = hi
        bl[rows, cols] = lo

    def pass_on(s):
        for way in range(2):
            ag_in(s, way).wait_recv()
            fw(s, way).start()

    bcopy.wait()

    @pl.loop(0, K // 128)
    def _(i):
        split(bown, i, c)

    pass_on(0)

    for i in range(PIECES):
        bs(i).wait_recv()

    @pl.loop(0, K // 128)
    def _(i):
        split(bsib, i, 1 - c)

    def split_rows(s):
        a = apan[s].reshape(16 * R, K)
        hi = a.astype(jnp.bfloat16)
        both[: 16 * R] = hi
        both[16 * R :] = (a - hi.astype(jnp.float32)).astype(jnp.bfloat16)

    def multiply(u, i):
        for half in range(2):
            cols = pl.ds(pl.multiple_of(half * K + i * W, W), W)
            two = jnp.dot(both[...], bh[:, cols], preferred_element_type=jnp.float32)
            acc = jnp.dot(both[: 16 * R], bl[:, cols], preferred_element_type=jnp.float32)
            acc = (two[: 16 * R] + (two[16 * R :] + acc)).reshape(4, 4, R, W)
            if half == 0:
                p[u, 0] = acc
            else:
                for n in range(4):
                    p[u, 1, :, n] = acc[n]

    def exchange(u):
        @pl.when(zl == c)
        def _():
            zsib(u).start()

        @pl.when(zl != c)
        def _():
            for h in range(2):
                zfar(u, h).start()

    def finish(u):
        cols = pl.ds(pl.multiple_of((u % UN) * W, W), W)

        @pl.when(zl == c)
        def _():
            arrived(zr.at[u, 0], zrs.at[u])
            o_ref[u // UN, :, cols] = red[u, c] + zr[u, 0]

        @pl.when(zl != c)
        def _():
            arrived(zr.at[u], zrs.at[u])
            o_ref[u // UN, :, cols] = zr[u, 0] + zr[u, 1]

    @pl.loop(0, U + 4 * LAG)
    def _(u):
        i = u % UN
        s = u // UN

        @pl.when((i == 0) & (s < T))
        def _():
            @pl.when(s + AHEAD < T)
            def _():
                for way in range(2):
                    ag(s + AHEAD, way).start()

            @pl.when(s + 1 < T)
            def _():
                pass_on(s + 1)

            own_copy(s).wait()
            fw_in(s).wait_recv()
            split_rows(s)

        @pl.when(u == (T - 1) * UN)
        def _():
            @pl.loop(0, HELD)
            def _(t):
                exchange(t)

        @pl.when(u < U)
        def _():
            multiply(u, i)
            for k, w in PAIRS:
                send_a(u, k, w).start()
            for k, w in PAIRS:
                send_b(u, k, w).start()

        @pl.when((u >= LAG) & (u < U + LAG))
        def _():
            t = u - LAG
            arrived(ra.at[t], ar.at[t])
            for k, w in PAIRS:
                m[t, k, w] = p[t, k, ring(at1[k], HOPS[w]), 2 * w : 2 * w + 2] + ra[t, k, w]
                send_c(t, k, w).start()

        @pl.when((u >= 2 * LAG) & (u < U + 2 * LAG))
        def _():
            t = u - 2 * LAG
            arrived(rbc.at[t], bcr.at[t])
            for k in range(2):
                for w in range(2):
                    part = slice(2 * w, 2 * w + 2)
                    q[t, k, part] = p[t, k, at1[k], part] + (rbc[t, 0, k, 1 - w] + rbc[t, 1, k, w])
                for i2 in range(3):
                    send_2(t, k, i2).start()

        @pl.when(u == U - 1 + 2 * LAG)
        def _():
            @pl.loop(0, HELD)
            def _(t):
                finish(t)

        @pl.when((u >= 3 * LAG) & (u < U + 3 * LAG))
        def _():
            t = u - 3 * LAG
            arrived(r2.at[t], st2r.at[t])
            for k in range(2):
                red[t, k] = (q[t, k, at2[k]] + r2[t, k, 0]) + (r2[t, k, 1] + r2[t, k, 2])

            @pl.when(t >= HELD)
            def _():
                exchange(t)

        @pl.when(u >= HELD + 4 * LAG)
        def _():
            finish(u - 4 * LAG)

    sent(bsib, bss)
    for way in range(2):
        sent(apan.at[:, 0], ags.at[way])
        sent(apan.at[:, 0, pl.ds(0, 2)], fws.at[way])
    sent(ra, as_)
    sent(rbc.at[:, 0], bs_)
    sent(m, cs)
    sent(r2, st2s)

    @pl.when(zl == c)
    def _():
        sent(red.at[:, 0], zs)

    @pl.when(zl != c)
    def _():
        sent(red, zs)


def ladder(a, b):
    f32, bf16 = jnp.float32, jnp.bfloat16
    dma = pltpu.SemaphoreType.DMA
    return pl.pallas_call(
        kernel,
        out_shape=jax.ShapeDtypeStruct((T, R, K), f32),
        in_specs=[pl.BlockSpec(memory_space=pl.ANY)] * 2,
        out_specs=pl.BlockSpec(memory_space=pltpu.VMEM),
        scratch_shapes=[
            pltpu.VMEM((T, 4, 4, R, K), f32),
            pltpu.VMEM((K, K), f32),
            pltpu.VMEM((K, K), f32),
            pltpu.VMEM((K, 2 * K), bf16),
            pltpu.VMEM((K, 2 * K), bf16),
            pltpu.VMEM((32 * R, K), bf16),
            pltpu.VMEM((U, 2, 4, 4, R, W), f32),
            pltpu.VMEM((U, 2, 2, 2, R, W), f32),
            pltpu.VMEM((U, 2, 2, 2, 2, R, W), f32),
            pltpu.VMEM((U, 2, 2, 2, R, W), f32),
            pltpu.VMEM((U, 2, 4, R, W), f32),
            pltpu.VMEM((U, 2, 3, R, W), f32),
            pltpu.VMEM((U, 2, R, W), f32),
            pltpu.VMEM((U, 2, R, W), f32),
            dma((T,)), dma, dma, dma((PIECES,)),
            dma((2,)), dma((2, T)), dma((2,)), dma((T,)),
            dma, dma((U,)), dma, dma, dma((U,)), dma, dma((U,)), dma, dma((U,)),
        ],
        cost_estimate=pl.CostEstimate(flops=2 * 1152 * 2048 * 1024 * 3, bytes_accessed=8 * 2**20, transcendentals=0),
        compiler_params=pltpu.CompilerParams(collective_id=0, has_side_effects=True, vmem_limit_bytes=52 * 2**20),
    )(a, b)


def shards(amplitudes, integrals, residual_in):
    owned = ladder(amplitudes.reshape(4, T, R, K), integrals)
    return residual_in + owned.reshape(72, K)


def solution(mesh):
    placed = (P("cols", "depth"), P("depth", "cols"), P("depth", "cols"))
    return jax.shard_map(
        shards, mesh=mesh, in_specs=placed, out_specs=P("depth", "cols"), check_vma=False
    )
```

time: 335 us -> 116 us (0.35)
  the two profiles are of different devices: /device:TPU:64 before, /device:TPU:1 now
where the time goes in v2:
time: 116 us
  Pallas kernels  114 us (98%)
  local copies, waits for them, and re-layouts  1.27 us (1%)
    pallas_call x1, Pallas kernels, ladder(): pl.pallas_call(kernel, out_shape=jax.ShapeDtypeStruct((T, R, K), f32), in...  114 us

profile of v2, /device:TPU:1, one launch (start us, length us, event | category | flops | bytes accessed | tf_op | source)
XLA Modules:
  0.0 115.7 jit_solution(1455698748871527879)
XLA Ops:
  0.0 0.0 copy-start
  0.0 1.3 %copy-done = f32[288,1024]{1,0:T(8,128)S(1)} copy-done((f32[288,1024]{1,0:T(8,128)S(1)}, f32[288,1024]{1,0:T(8,128)}, u32[]{:S(2)}) %copy-start) | copy-done | bytes 1179672
  1.3 0.0 copy-start.1
  1.3 113.7 %shard_map.37 = f32[9,8,1024]{2,1,0:T(8,128)S(1)} custom-call(f32[4,9,8,1024]{3,2,1,0:T(8,128)S(1)} %bitcast.3, f32[1024,1024]{1,0:T(8,128)} %b_ref.1), custom_call_target="tpu_custom_call" | custom-call | flops 14495514624 | bytes 8388608 | tf_op jit(solution)/shard_map/pallas_call | solution.py:284
  114.9 0.0 copy-done.1
  115.0 0.7 bitcast_add_fusion
Async XLA Ops:
  0.0 1.3 %copy-start = (f32[288,1024]{1,0:T(8,128)S(1)}, f32[288,1024]{1,0:T(8,128)}, u32[]{:S(2)}) copy-start(f32[288,1024]{1,0:T(8,128)} %param.3) | copy-start | bytes 3538948
  1.3 113.7 %copy-start.1 = (f32[72,1024]{1,0:T(8,128)S(1)}, f32[72,1024]{1,0:T(8,128)}, u32[]{:S(2)}) copy-start(f32[72,1024]{1,0:T(8,128)} %param.5) | copy-start | bytes 884740

commit v3 on v2

--- a/solution.py
+++ b/solution.py
@@ -14,7 +14,7 @@
 W = K // UN
 U = T * UN
 LAG = 2
-HELD = (T - 1) * UN - 3 * LAG
+HELD = 4
 PIECES = 4
 HOPS = (1, -1, 2)
 

time: 116 us -> 114 us (0.983)
  Pallas kernels: 114 us -> 112 us
    pallas_call x1, Pallas kernels: 114 us -> 112 us  [ladder(): pl.pallas_call(kernel, out_shape=jax.ShapeDtypeStruct((T, R, K), f32), in...]
where the time goes in v3:
time: 114 us
  Pallas kernels  112 us (98%)
  local copies, waits for them, and re-layouts  1.27 us (1%)
    pallas_call x1, Pallas kernels, ladder(): pl.pallas_call(kernel, out_shape=jax.ShapeDtypeStruct((T, R, K), f32), in...  112 us

profile of v3, /device:TPU:1, one launch (start us, length us, event | category | flops | bytes accessed | tf_op | source)
XLA Modules:
  0.0 113.6 jit_solution(14352590574423168777)
XLA Ops:
  0.0 0.0 copy-start
  0.0 1.3 %copy-done = f32[288,1024]{1,0:T(8,128)S(1)} copy-done((f32[288,1024]{1,0:T(8,128)S(1)}, f32[288,1024]{1,0:T(8,128)}, u32[]{:S(2)}) %copy-start) | copy-done | bytes 1179672
  1.3 0.0 copy-start.1
  1.3 111.5 %shard_map.37 = f32[9,8,1024]{2,1,0:T(8,128)S(1)} custom-call(f32[4,9,8,1024]{3,2,1,0:T(8,128)S(1)} %bitcast.3, f32[1024,1024]{1,0:T(8,128)} %b_ref.1), custom_call_target="tpu_custom_call" | custom-call | flops 14495514624 | bytes 8388608 | tf_op jit(solution)/shard_map/pallas_call | solution.py:284
  112.8 0.0 copy-done.1
  112.8 0.7 bitcast_add_fusion
Async XLA Ops:
  0.0 1.3 %copy-start = (f32[288,1024]{1,0:T(8,128)S(1)}, f32[288,1024]{1,0:T(8,128)}, u32[]{:S(2)}) copy-start(f32[288,1024]{1,0:T(8,128)} %param.3) | copy-start | bytes 3538948
  1.3 111.6 %copy-start.1 = (f32[72,1024]{1,0:T(8,128)S(1)}, f32[72,1024]{1,0:T(8,128)}, u32[]{:S(2)}) copy-start(f32[72,1024]{1,0:T(8,128)} %param.5) | copy-start | bytes 884740

commit v4 on v3

--- a/solution.py
+++ b/solution.py
@@ -307,7 +307,7 @@
         ],
         cost_estimate=pl.CostEstimate(flops=2 * 1152 * 2048 * 1024 * 3, bytes_accessed=8 * 2**20, transcendentals=0),
         compiler_params=pltpu.CompilerParams(collective_id=0, has_side_effects=True, vmem_limit_bytes=52 * 2**20),
-    )(a, b)
+    )(pltpu.with_memory_space_constraint(a, pltpu.HBM), b)
 
 
 def shards(amplitudes, integrals, residual_in):

time: 114 us -> 113 us (level)
  local copies, waits for them, and re-layouts: 1.27 us -> 0.01 us
    unnamed x4 -> x2, local copies, waits for them, and re-layouts: 1.27 us -> 0.01 us
where the time goes in v4:
time: 113 us
  Pallas kernels  112 us (99%)
    pallas_call x1, Pallas kernels, ladder(): pl.pallas_call(kernel, out_shape=jax.ShapeDtypeStruct((T, R, K), f32), in...  112 us

profile of v4, /device:TPU:1, one launch (start us, length us, event | category | flops | bytes accessed | tf_op | source)
XLA Modules:
  0.0 113.1 jit_solution(8058642805827657021)
XLA Ops:
  0.0 0.0 copy-start
  0.0 112.3 %shard_map.37 = f32[9,8,1024]{2,1,0:T(8,128)S(1)} custom-call(f32[4,9,8,1024]{3,2,1,0:T(8,128)} %bitcast.3, f32[1024,1024]{1,0:T(8,128)} %b_ref.1), custom_call_target="tpu_custom_call" | custom-call | flops 14495514624 | bytes 8388608 | tf_op jit(solution)/shard_map/pallas_call | solution.py:284
  112.3 0.0 copy-done
  112.3 0.7 bitcast_add_fusion
Async XLA Ops:
  0.0 112.3 %copy-start = (f32[72,1024]{1,0:T(8,128)S(1)}, f32[72,1024]{1,0:T(8,128)}, u32[]{:S(2)}) copy-start(f32[72,1024]{1,0:T(8,128)} %param.5) | copy-start | bytes 884740
